TPU v7x, 32 devices: a whole 2x2x4 slice. The times are simulated.
32 devices in a mesh: blk: 16 (over z, x, core), rep: 2 (over y).
Axes of the slice: x: 2, y: 2, z: 4, core: 2. Of those that a mesh axis runs over, the one named last changes fastest.
Arguments:
- features: bfloat16 [4096, 128], P(('blk', 'rep')), may hold values from -6 to 6
- tile_mask: int32 [32, 32], P('blk'), may hold values 0 or 1
- multiplicity: int32 [32, 32], P('blk'), may hold values from 1 to 4
- w_query: bfloat16 [128, 128], replicated, may hold values from -0.5 to 0.5
- w_value: bfloat16 [128, 128], replicated, may hold values from -0.5 to 0.5
Outputs:
- updated: bfloat16 [4096, 128], P(('blk', 'rep'))
All inputs are finite; a program needn't handle non-finite values. No bound on the sum of `tile_mask` on one device may be relied on, other than what follows from the above.
Results may differ from a plain program's by a relative error of at most 0.0057.
Values may be sent and summed in bfloat16 or wider, within the bound.
A program may use at most 64 MiB of HBM per device.

v0:
```python
import math
import jax
import jax.numpy as jnp
from jax import lax
from jax.sharding import PartitionSpec as P

TILE = 128


def body(features, tile_mask, multiplicity, w_query, w_value):
    src_rows = features.shape[0]
    cycle_count = lax.axis_size("blk")
    rep_count = lax.axis_size("rep")
    rep_index = lax.axis_index("rep")
    own_query = jnp.dot(features, w_query, preferred_element_type=jnp.float32).astype(jnp.bfloat16)
    queries = lax.all_gather(own_query, "rep", axis=0, tiled=True)
    tgt_rows = queries.shape[0]
    tgt_tiles = tgt_rows // TILE
    src_tiles = src_rows // TILE
    factor = (tile_mask * multiplicity).astype(jnp.float32)
    factor = factor.reshape(tgt_tiles, cycle_count, rep_count, src_tiles)
    factor = lax.dynamic_index_in_dim(factor, rep_index, 2, keepdims=False)
    root_scale = 1.0 / features.shape[1] ** 0.5

    def absorb_tiles(partial_value, source, tile_factor):
        count_rows = source.shape[0]
        scores = (
            lax.dot_general(
                queries, source, (((1,), (1,)), ((), ())), preferred_element_type=jnp.float32
            )
            * root_scale
        )
        scores = jnp.where(scores > 0, scores, 0.2 * scores)
        weights = (
            scores.reshape(tgt_tiles, TILE, count_rows // TILE, TILE)
            * tile_factor[:, None, :, None]
        )
        weights = weights.reshape(tgt_rows, count_rows).astype(jnp.bfloat16)
        return partial_value + jnp.dot(weights, source, preferred_element_type=jnp.float32)

    start = jnp.zeros((tgt_rows, features.shape[1]), jnp.float32)
    flat_factor = factor.reshape(tgt_tiles, cycle_count * src_tiles)
    piece = lax.all_gather(features, "blk", axis=0, tiled=True)
    piece_rows = piece.shape[0]
    step_rows = math.gcd(piece_rows, max(src_rows, 1024))
    step_count = piece_rows // step_rows
    piece_blocks = piece.reshape(step_count, step_rows, piece.shape[1])

    def one_part(carry, index_pair):
        part_rows, part_index = index_pair
        first_tile = part_index * step_rows // TILE
        tile_factor = lax.dynamic_slice_in_dim(flat_factor, first_tile, step_rows // TILE, 1)
        return (absorb_tiles(carry, part_rows, tile_factor), None)

    result, unused = lax.scan(
        one_part, start, (piece_blocks, jnp.arange(step_count, dtype=jnp.int32))
    )
    partial_value = result
    summed = lax.psum_scatter(partial_value, "rep", scatter_dimension=0, tiled=True)
    total_verts = src_rows * cycle_count * rep_count
    aggregate = (summed * (2.0 * total_verts) ** (-0.5)).astype(jnp.bfloat16)
    mixed = jnp.dot(aggregate, w_value, preferred_element_type=jnp.float32)
    return (features.astype(jnp.float32) + mixed).astype(jnp.bfloat16)


def solution(mesh):
    in_specs = (P(("blk", "rep"), None), P("blk", None), P("blk", None), P(), P())
    out_specs = P(("blk", "rep"), None)
    return jax.shard_map(body, mesh=mesh, in_specs=in_specs, out_specs=out_specs, check_vma=False)
```

profile of v0, /device:TPU:0, one launch (start us, length us, event | category | flops | bytes accessed | tf_op | source)
XLA Modules:
  0.0 58.8 jit_solution(14389451639451653202)
XLA Ops:
  6.5 0.0 copy-start
  6.5 0.0 reduce-scatter.2.cloned.1.call-start
  6.5 0.0 copy-start.5
  6.5 0.0 copy-start.4
  6.6 0.7 %copy-done.5 = s32[2,32]{1,0:T(2,128)S(1)} copy-done((s32[2,32]{1,0:T(2,128)S(1)}, s32[2,32]{1,0:T(2,128)}, u32[]{:S(2)}) %copy-start.5) | copy-done | bytes 280
  7.2 0.0 copy-done.4
  7.3 0.1 reshape.20
  7.3 0.0 copy-start.1
  7.3 0.1 constant_dynamic-slice_fusion.1
  7.4 0.2 copy.8
  7.6 0.5 copy-done.1
  8.1 24.6 %all_gather.6 = bf16[2048,128]{1,0:T(8,128)(2,1)S(1)} all-gather(bf16[128,128]{1,0:T(8,128)(2,1)S(1)} %copy-done.1), channel_id=1, replica_groups=mesh['blk'=16,'rep'=2] {'blk'}, dimensions={0}, use_global_device_ids=true | all-gather | bytes 557056 | tf_op jit(solution)/shard_map/all_gather | solution.py:43
  32.7 0.0 copy-done
  32.7 0.1 convolution_convert_fusion
  32.8 4.6 %all_gather.7 = bf16[256,128]{1,0:T(8,128)(2,1)S(1)} all-gather(bf16[128,128]{1,0:T(8,128)(2,1)S(1)} %convolution_convert_fusion), channel_id=1, replica_groups=mesh['blk'=16,'rep'=2] {'rep'}, dimensions={0}, use_global_device_ids=true | all-gather | bytes 98304 | tf_op jit(solution)/shard_map/all_gather | solution.py:16
  37.4 4.4 %while.13 = (s32[]{:T(128)}, f32[256,128]{1,0:T(8,128)S(1)}, bf16[2,1024,128]{2,1,0:T(8,128)(2,1)S(1)}, bf16[256,128]{1,0:T(8,128)(2,1)S(1)}, s32[2]{0:T(128)S(1...) while((s32[]{:T(128)}, f32[256,128]{1,0:T(8,128)S(1)}, ...), condition=%wide.region_1.2_spmd.clone, body=%wide.region_0.1_spmd.clone.sunk | while | flops 135856144 | bytes 2950683 | solution.py:55
  37.4 0.6 dynamic_slice.44
  38.6 0.3 mul.98
  38.9 0.7 %convolution_add_fusion.3 = f32[256,128]{1,0:T(8,128)S(1)} fusion(f32[128,8,2,128]{3,2,1,0:T(2,128)S(1)} %bitcast.43, bf16[256,128]{1,0:T(8,128)(2,1)S(1)} %get-tuple-element.196, bf16[2,1024,128]{2,1,0:T(8,128)(2,1)S(1)} %get-tuple-element.195, s32[]{:T(128)} %get-tuple-element.180, f32[256,128]{1,0:T(8,128)S(1)} %get-tuple-element.181, pred[]{:T(512)S(6)} %compare.9), kind=kOutput, calls=%fused_computation.1.clone.1 | convolution fusion | flops 135856128 | bytes 1901569 | tf_op jit(solution)/shard_map/while/body/eval_jaxpr/dot_general | solution.py:39
  39.6 0.6 dynamic_slice.44
  40.8 0.3 mul.98
  41.2 0.7 %convolution_add_fusion.3 = f32[256,128]{1,0:T(8,128)S(1)} fusion(f32[128,8,2,128]{3,2,1,0:T(2,128)S(1)} %bitcast.43, bf16[256,128]{1,0:T(8,128)(2,1)S(1)} %get-tuple-element.196, bf16[2,1024,128]{2,1,0:T(8,128)(2,1)S(1)} %get-tuple-element.195, s32[]{:T(128)} %get-tuple-element.180, f32[256,128]{1,0:T(8,128)S(1)} %get-tuple-element.181, pred[]{:T(512)S(6)} %compare.9), kind=kOutput, calls=%fused_computation.1.clone.1 | convolution fusion | flops 135856128 | bytes 1901569 | tf_op jit(solution)/shard_map/while/body/eval_jaxpr/dot_general | solution.py:39
  41.8 0.0 copy-start.2
  41.9 0.0 copy-start.3
  41.9 0.6 %copy-done.2 = f32[256,128]{1,0:T(8,128)} copy-done((f32[256,128]{1,0:T(8,128)}, f32[256,128]{1,0:T(8,128)S(1)}, u32[]{:S(2)}) %copy-start.2) | copy-done | bytes 131096
  42.5 0.0 reduce-scatter.2.cloned.1.call-update
  42.5 7.8 %reduce-scatter.2.cloned.1.call-done = f32[128,128]{1,0:T(8,128)} async-done(((f32[256,128]{1,0:T(8,128)}), f32[128,128]{1,0:T(8,128)}) %reduce-scatter.2.cloned.1.call-update) | async-done | bytes 65552 | tf_op jit(solution)/shard_map/reduce_scatter | solution.py:59
  50.3 0.0 copy-done.3
  50.3 1.6 %fusion.14 = bf16[128,128]{1,0:T(8,128)(2,1)} fusion(bf16[128,128]{1,0:T(8,128)(2,1)S(1)} %copy-done.3, bf16[128,128]{1,0:T(8,128)(2,1)S(1)} %copy-done.1, f32[128,128]{1,0:T(8,128)} %reduce-scatter.2.cloned.1.call-done), kind=kOutput, calls=%fused_computation.15 | convolution fusion | flops 4276224 | bytes 163840 | tf_op jit(solution)/shard_map/dot_general | solution.py:62
  (5 shorter events, 0.0 us)
Async XLA Ops:
  6.5 26.2 %copy-start = (bf16[128,128]{1,0:T(8,128)(2,1)S(1)}, bf16[128,128]{1,0:T(8,128)(2,1)}, u32[]{:S(2)}) copy-start(bf16[128,128]{1,0:T(8,128)(2,1)} %param.10) | copy-start | bytes 98308
  6.5 43.8 %reduce-scatter.2.cloned.1.call-start = ((), (), s32[]{:S(2)}) async-start(), calls=%async_computation.1 | async-start | bytes 196608 | tf_op jit(solution)/shard_map/reduce_scatter | solution.py:59
  6.5 0.7 %copy-start.5 = (s32[2,32]{1,0:T(2,128)S(1)}, s32[2,32]{1,0:T(2,128)}, u32[]{:S(2)}) copy-start(s32[2,32]{1,0:T(2,128)} %param.9) | copy-start | bytes 772
  6.5 0.7 %copy-start.4 = (s32[2,32]{1,0:T(2,128)S(1)}, s32[2,32]{1,0:T(2,128)}, u32[]{:S(2)}) copy-start(s32[2,32]{1,0:T(2,128)} %param.8) | copy-start | bytes 772
  7.3 0.8 %copy-start.1 = (bf16[128,128]{1,0:T(8,128)(2,1)S(1)}, bf16[128,128]{1,0:T(8,128)(2,1)}, u32[]{:S(2)}) copy-start(bf16[128,128]{1,0:T(8,128)(2,1)} %param.7) | copy-start | bytes 98308
  41.8 0.7 %copy-start.2 = (f32[256,128]{1,0:T(8,128)}, f32[256,128]{1,0:T(8,128)S(1)}, u32[]{:S(2)}) copy-start(f32[256,128]{1,0:T(8,128)S(1)} %get-tuple-element.84) | copy-start | bytes 393220
  41.9 8.5 %copy-start.3 = (bf16[128,128]{1,0:T(8,128)(2,1)S(1)}, bf16[128,128]{1,0:T(8,128)(2,1)}, u32[]{:S(2)}) copy-start(bf16[128,128]{1,0:T(8,128)(2,1)} %param.11) | copy-start | bytes 98308
Sparse Core Ops, SparseCore 0:
  42.6 7.6 reduce-scatter.1
where the time goes:
time: 59.1 us; the launch traced here: 58.8 us
  blocking collectives  29.2 us (49%)
  between operations  13.4 us (23%)
  waiting for transfers between devices  7.82 us (13%)
  local copies, waits for them, and re-layouts  4.05 us (7%)
  matrix products  3.05 us (5%)
  loops' own time  1.24 us (2%)
    all_gather x1, blocking collectives, body(): piece = lax.all_gather(features, 'blk', axis=0, tiled=True)  24.6 us
    reduce_scatter x1, waiting for transfers between devices, body(): lax.psum_scatter(partial_value, 'rep', scatter_dimension=0, tiled=True)  7.8 us
    all_gather x1, blocking collectives, body(): queries = lax.all_gather(own_query, 'rep', axis=0, tiled=True)  4.58 us
    unnamed x13, local copies, waits for them, and re-layouts  2.02 us
    dot_general x1, matrix products, body(): mixed = jnp.dot(aggregate, w_value, preferred_element_type=jnp.float32)  1.59 us
    dot_general x2, matrix products, absorb_tiles(): jnp.dot(weights, source, preferred_element_type=jnp.float32)  1.33 us
    another operation x1, loops' own time, body(): lax.scan(one_part, start, (piece_blocks, jnp.arange(step_count, dtype=jnp...  1.24 us
  transfers between devices with their start and end apart: 1, of which 1 were waited for; matrix products, arithmetic and copies ran while one was open for 0% of the time, Pallas kernels for 0%

commit v1 on v0

--- a/solution.py
+++ b/solution.py
@@ -40,7 +40,15 @@
 
     start = jnp.zeros((tgt_rows, features.shape[1]), jnp.float32)
     flat_factor = factor.reshape(tgt_tiles, cycle_count * src_tiles)
-    piece = lax.all_gather(features, "blk", axis=0, tiled=True)
+    near, raw_out, newest = (lax.psum(1, axis_name="blk"), lax.axis_index("blk"), features.shape[0])
+    sheets = tuple(((kk, (kk + 1) % near) for kk in range(near)))
+    piece = jnp.zeros((*features.shape[:0], near * newest, *features.shape[1:]), features.dtype)
+    back = features
+    for m in range(near):
+        finding = (raw_out - m) % near
+        piece = lax.dynamic_update_slice_in_dim(piece, back, finding * newest, axis=0)
+        if m < near - 1:
+            back = lax.ppermute(back, perm=sheets, axis_name="blk")
     piece_rows = piece.shape[0]
     step_rows = math.gcd(piece_rows, max(src_rows, 1024))
     step_count = piece_rows // step_rows

time: 59.1 us -> 121 us (2.05)
  waiting for transfers between devices: 7.82 us -> 91.9 us
  blocking collectives: 29.2 us -> 5.07 us
  starting transfers between devices: 0.01 us -> 1.38 us
    ppermute x0 -> x15, waiting for transfers between devices: none -> 83.6 us  [body(): back = lax.ppermute(back, perm=sheets, axis_name='blk')]
    all_gather x1 -> x0, blocking collectives: 24.6 us -> none  [body(): piece = lax.all_gather(features, 'blk', axis=0, tiled=True)]
    ppermute x0 -> x15, starting transfers between devices: none -> 1.37 us  [body(): back = lax.ppermute(back, perm=sheets, axis_name='blk')]
  transfers between devices with their start and end apart: 1 -> 16, of which waited for: 1 -> 16; matrix products, arithmetic and copies ran while one was open for 0% -> 1% of each run, Pallas kernels for 0% -> 0%
where the time goes in v1:
time: 121 us; the launch traced here: 120 us
  waiting for transfers between devices  91.9 us (76%)
  between operations  13.8 us (11%)
  blocking collectives  5.07 us (4%)
  local copies, waits for them, and re-layouts  3.86 us (3%)
  matrix products  3.07 us (3%)
  loops' own time  1.4 us (1%)
  starting transfers between devices  1.38 us (1%)
    ppermute x15, waiting for transfers between devices, body(): back = lax.ppermute(back, perm=sheets, axis_name='blk')  83.6 us
    reduce_scatter x1, waiting for transfers between devices, body(): lax.psum_scatter(partial_value, 'rep', scatter_dimension=0, tiled=True)  8.25 us
    all_gather x1, blocking collectives, body(): queries = lax.all_gather(own_query, 'rep', axis=0, tiled=True)  5.07 us
  transfers between devices with their start and end apart: 16, of which 16 were waited for; matrix products, arithmetic and copies ran while one was open for 1% of the time, Pallas kernels for 0%

profile of v1, /device:TPU:0, one launch (start us, length us, event | category | flops | bytes accessed | tf_op | source)
XLA Modules:
  0.0 120.4 jit_solution(10581171954243351530)
XLA Ops:
  6.5 0.0 copy-start
  6.5 0.0 copy-start.1
  6.5 0.0 reduce-scatter.2.cloned.1.call-start
  6.5 0.5 collective-permute-start
  7.0 0.0 copy-start.5
  7.0 0.0 copy-start.4
  7.0 0.7 copy-done.5
  7.7 0.0 copy-done.4
  7.7 0.1 reshape.20
  7.8 0.0 copy-done
  7.8 0.0 copy-done.1
  7.8 0.1 convolution_convert_fusion
  8.0 0.1 broadcast_in_dim.8
  8.1 0.1 constant_dynamic-slice_fusion.1
  8.4 0.2 copy.8
  8.6 5.1 %all_gather.3 = bf16[256,128]{1,0:T(8,128)(2,1)S(1)} all-gather(bf16[128,128]{1,0:T(8,128)(2,1)S(1)} %convolution_convert_fusion), channel_id=1, replica_groups=mesh['blk'=16,'rep'=2] {'rep'}, dimensions={0}, use_global_device_ids=true | all-gather | bytes 98304 | tf_op jit(solution)/shard_map/all_gather | solution.py:16
  13.7 0.1 collective-permute-done
  13.8 0.8 collective-permute-start.1
  14.7 5.2 %collective-permute-done.1 = bf16[128,128]{1,0:T(8,128)(2,1)S(1)} collective-permute-done((bf16[128,128]{1,0:T(8,128)(2,1)S(1)}, bf16[128,128]{1,0:T(8,128)(2,1)S(1)}, u32[]{:S(2)}, u32[]{:S(2)}) %collective-permute-start.1) | collective-permute-done | bytes 32800 | tf_op jit(solution)/shard_map/ppermute | solution.py:51
  19.9 0.0 collective-permute-start.2
  19.9 6.0 %collective-permute-done.2 = bf16[128,128]{1,0:T(8,128)(2,1)S(1)} collective-permute-done((bf16[128,128]{1,0:T(8,128)(2,1)S(1)}, bf16[128,128]{1,0:T(8,128)(2,1)S(1)}, u32[]{:S(2)}, u32[]{:S(2)}) %collective-permute-start.2) | collective-permute-done | bytes 32800 | tf_op jit(solution)/shard_map/ppermute | solution.py:51
  25.9 0.0 collective-permute-start.3
  25.9 6.0 %collective-permute-done.3 = bf16[128,128]{1,0:T(8,128)(2,1)S(1)} collective-permute-done((bf16[128,128]{1,0:T(8,128)(2,1)S(1)}, bf16[128,128]{1,0:T(8,128)(2,1)S(1)}, u32[]{:S(2)}, u32[]{:S(2)}) %collective-permute-start.3) | collective-permute-done | bytes 32800 | tf_op jit(solution)/shard_map/ppermute | solution.py:51
  31.9 0.0 collective-permute-start.4
  31.9 6.0 %collective-permute-done.4 = bf16[128,128]{1,0:T(8,128)(2,1)S(1)} collective-permute-done((bf16[128,128]{1,0:T(8,128)(2,1)S(1)}, bf16[128,128]{1,0:T(8,128)(2,1)S(1)}, u32[]{:S(2)}, u32[]{:S(2)}) %collective-permute-start.4) | collective-permute-done | bytes 32800 | tf_op jit(solution)/shard_map/ppermute | solution.py:51
  38.0 0.0 collective-permute-start.5
  38.0 6.0 %collective-permute-done.5 = bf16[128,128]{1,0:T(8,128)(2,1)S(1)} collective-permute-done((bf16[128,128]{1,0:T(8,128)(2,1)S(1)}, bf16[128,128]{1,0:T(8,128)(2,1)S(1)}, u32[]{:S(2)}, u32[]{:S(2)}) %collective-permute-start.5) | collective-permute-done | bytes 32800 | tf_op jit(solution)/shard_map/ppermute | solution.py:51
  44.0 0.0 collective-permute-start.6
  44.0 6.0 %collective-permute-done.6 = bf16[128,128]{1,0:T(8,128)(2,1)S(1)} collective-permute-done((bf16[128,128]{1,0:T(8,128)(2,1)S(1)}, bf16[128,128]{1,0:T(8,128)(2,1)S(1)}, u32[]{:S(2)}, u32[]{:S(2)}) %collective-permute-start.6) | collective-permute-done | bytes 32800 | tf_op jit(solution)/shard_map/ppermute | solution.py:51
  50.0 0.0 collective-permute-start.7
  50.1 6.0 %collective-permute-done.7 = bf16[128,128]{1,0:T(8,128)(2,1)S(1)} collective-permute-done((bf16[128,128]{1,0:T(8,128)(2,1)S(1)}, bf16[128,128]{1,0:T(8,128)(2,1)S(1)}, u32[]{:S(2)}, u32[]{:S(2)}) %collective-permute-start.7) | collective-permute-done | bytes 32800 | tf_op jit(solution)/shard_map/ppermute | solution.py:51
  56.1 0.0 collective-permute-start.8
  56.1 6.0 %collective-permute-done.8 = bf16[128,128]{1,0:T(8,128)(2,1)S(1)} collective-permute-done((bf16[128,128]{1,0:T(8,128)(2,1)S(1)}, bf16[128,128]{1,0:T(8,128)(2,1)S(1)}, u32[]{:S(2)}, u32[]{:S(2)}) %collective-permute-start.8) | collective-permute-done | bytes 32800 | tf_op jit(solution)/shard_map/ppermute | solution.py:51
  62.1 0.0 collective-permute-start.9
  62.1 6.0 %collective-permute-done.9 = bf16[128,128]{1,0:T(8,128)(2,1)S(1)} collective-permute-done((bf16[128,128]{1,0:T(8,128)(2,1)S(1)}, bf16[128,128]{1,0:T(8,128)(2,1)S(1)}, u32[]{:S(2)}, u32[]{:S(2)}) %collective-permute-start.9) | collective-permute-done | bytes 32800 | tf_op jit(solution)/shard_map/ppermute | solution.py:51
  68.2 0.0 collective-permute-start.10
  68.2 6.0 %collective-permute-done.10 = bf16[128,128]{1,0:T(8,128)(2,1)S(1)} collective-permute-done((bf16[128,128]{1,0:T(8,128)(2,1)S(1)}, bf16[128,128]{1,0:T(8,128)(2,1)S(1)}, u32[]{:S(2)}, u32[]{:S(2)}) %collective-permute-start.10) | collective-permute-done | bytes 32800 | tf_op jit(solution)/shard_map/ppermute | solution.py:51
  74.2 0.0 collective-permute-start.11
  74.2 6.0 %collective-permute-done.11 = bf16[128,128]{1,0:T(8,128)(2,1)S(1)} collective-permute-done((bf16[128,128]{1,0:T(8,128)(2,1)S(1)}, bf16[128,128]{1,0:T(8,128)(2,1)S(1)}, u32[]{:S(2)}, u32[]{:S(2)}) %collective-permute-start.11) | collective-permute-done | bytes 32800 | tf_op jit(solution)/shard_map/ppermute | solution.py:51
  80.2 0.0 collective-permute-start.12
  80.2 6.0 %collective-permute-done.12 = bf16[128,128]{1,0:T(8,128)(2,1)S(1)} collective-permute-done((bf16[128,128]{1,0:T(8,128)(2,1)S(1)}, bf16[128,128]{1,0:T(8,128)(2,1)S(1)}, u32[]{:S(2)}, u32[]{:S(2)}) %collective-permute-start.12) | collective-permute-done | bytes 32800 | tf_op jit(solution)/shard_map/ppermute | solution.py:51
  86.3 0.0 collective-permute-start.13
  86.3 6.0 %collective-permute-done.13 = bf16[128,128]{1,0:T(8,128)(2,1)S(1)} collective-permute-done((bf16[128,128]{1,0:T(8,128)(2,1)S(1)}, bf16[128,128]{1,0:T(8,128)(2,1)S(1)}, u32[]{:S(2)}, u32[]{:S(2)}) %collective-permute-start.13) | collective-permute-done | bytes 32800 | tf_op jit(solution)/shard_map/ppermute | solution.py:51
  92.3 0.0 collective-permute-start.14
  92.3 6.0 %collective-permute-done.14 = bf16[128,128]{1,0:T(8,128)(2,1)S(1)} collective-permute-done((bf16[128,128]{1,0:T(8,128)(2,1)S(1)}, bf16[128,128]{1,0:T(8,128)(2,1)S(1)}, u32[]{:S(2)}, u32[]{:S(2)}) %collective-permute-start.14) | collective-permute-done | bytes 32800 | tf_op jit(solution)/shard_map/ppermute | solution.py:51
  98.4 4.7 %while.13 = (s32[]{:T(128)}, f32[256,128]{1,0:T(8,128)S(1)}, bf16[2,1024,128]{2,1,0:T(8,128)(2,1)S(1)}, bf16[256,128]{1,0:T(8,128)(2,1)S(1)}, s32[2]{0:T(128)S(1...) while((s32[]{:T(128)}, f32[256,128]{1,0:T(8,128)S(1)}, ...), condition=%wide.region_1.2_spmd.clone, body=%wide.region_0.1_spmd.clone.sunk | while | flops 135856144 | bytes 2950683 | solution.py:63
  98.4 0.6 dynamic_slice.44
  99.7 0.3 mul.162
  100.0 0.7 convolution_add_fusion.3
  100.7 0.6 dynamic_slice.44
  102.0 0.3 mul.162
  102.4 0.7 convolution_add_fusion.3
  103.0 0.0 copy-start.2
  103.1 0.0 copy-start.3
  103.1 0.6 copy-done.2
  103.7 0.0 reduce-scatter.2.cloned.1.call-update
  103.7 8.3 %reduce-scatter.2.cloned.1.call-done = f32[128,128]{1,0:T(8,128)} async-done(((f32[256,128]{1,0:T(8,128)}), f32[128,128]{1,0:T(8,128)}) %reduce-scatter.2.cloned.1.call-update) | async-done | bytes 65552 | tf_op jit(solution)/shard_map/reduce_scatter | solution.py:67
  112.0 0.0 copy-done.3
  112.0 1.6 %fusion.14 = bf16[128,128]{1,0:T(8,128)(2,1)} fusion(bf16[128,128]{1,0:T(8,128)(2,1)S(1)} %copy-done.3, bf16[128,128]{1,0:T(8,128)(2,1)S(1)} %copy-done.1, f32[128,128]{1,0:T(8,128)} %reduce-scatter.2.cloned.1.call-done), kind=kOutput, calls=%fused_computation.15 | convolution fusion | flops 4276224 | bytes 163840 | tf_op jit(solution)/shard_map/dot_general | solution.py:70
  (21 shorter events, 0.2 us)
Async XLA Ops:
  6.5 1.3 %copy-start = (bf16[128,128]{1,0:T(8,128)(2,1)S(1)}, bf16[128,128]{1,0:T(8,128)(2,1)}, u32[]{:S(2)}) copy-start(bf16[128,128]{1,0:T(8,128)(2,1)} %param.10) | copy-start | bytes 98308
  6.5 1.3 %copy-start.1 = (bf16[128,128]{1,0:T(8,128)(2,1)S(1)}, bf16[128,128]{1,0:T(8,128)(2,1)}, u32[]{:S(2)}) copy-start(bf16[128,128]{1,0:T(8,128)(2,1)} %param.7) | copy-start | bytes 98308
  6.5 105.4 %reduce-scatter.2.cloned.1.call-start = ((), (), s32[]{:S(2)}) async-start(), calls=%async_computation.1 | async-start | bytes 196608 | tf_op jit(solution)/shard_map/reduce_scatter | solution.py:67
  6.5 7.3 %collective-permute-start = (bf16[128,128]{1,0:T(8,128)(2,1)}, bf16[128,128]{1,0:T(8,128)(2,1)S(1)}, u32[]{:S(2)}, u32[]{:S(2)}) collective-permute-start(bf16[128,128]{1,0:T(8,128)(2,1)} %param.7), channel_id=1, source_target_pairs={{0,2},{2,4},{4,6},{6,8},{8,10},{10,12},{12,14},{14,16},{16,18},{18... | collective-permute-start | bytes 98312 | tf_op jit(solution)/shard_map/ppermute | solution.py:51
  7.0 0.7 copy-start.5
  7.0 0.7 copy-start.4
  13.8 6.0 %collective-permute-start.1 = (bf16[128,128]{1,0:T(8,128)(2,1)S(1)}, bf16[128,128]{1,0:T(8,128)(2,1)S(1)}, u32[]{:S(2)}, u32[]{:S(2)}) collective-permute-start(bf16[128,128]{1,0:T(8,128)(2,1)S(1)} %collective-permute-done), channel_id=1, source_target_pairs={{0,2},{2,4},{4,6},{6,8},{8,10},{10,12},{12,14},{14,16},{16,18},{18... | collective-permute-start | bytes 98312 | tf_op jit(solution)/shard_map/ppermute | solution.py:51
  19.9 6.0 %collective-permute-start.2 = (bf16[128,128]{1,0:T(8,128)(2,1)S(1)}, bf16[128,128]{1,0:T(8,128)(2,1)S(1)}, u32[]{:S(2)}, u32[]{:S(2)}) collective-permute-start(bf16[128,128]{1,0:T(8,128)(2,1)S(1)} %collective-permute-done.1), channel_id=1, source_target_pairs={{0,2},{2,4},{4,6},{6,8},{8,10},{10,12},{12,14},{14,16},{16,18},{18... | collective-permute-start | bytes 98312 | tf_op jit(solution)/shard_map/ppermute | solution.py:51
  25.9 6.0 %collective-permute-start.3 = (bf16[128,128]{1,0:T(8,128)(2,1)S(1)}, bf16[128,128]{1,0:T(8,128)(2,1)S(1)}, u32[]{:S(2)}, u32[]{:S(2)}) collective-permute-start(bf16[128,128]{1,0:T(8,128)(2,1)S(1)} %collective-permute-done.2), channel_id=1, source_target_pairs={{0,2},{2,4},{4,6},{6,8},{8,10},{10,12},{12,14},{14,16},{16,18},{18... | collective-permute-start | bytes 98312 | tf_op jit(solution)/shard_map/ppermute | solution.py:51
  31.9 6.0 %collective-permute-start.4 = (bf16[128,128]{1,0:T(8,128)(2,1)S(1)}, bf16[128,128]{1,0:T(8,128)(2,1)S(1)}, u32[]{:S(2)}, u32[]{:S(2)}) collective-permute-start(bf16[128,128]{1,0:T(8,128)(2,1)S(1)} %collective-permute-done.3), channel_id=1, source_target_pairs={{0,2},{2,4},{4,6},{6,8},{8,10},{10,12},{12,14},{14,16},{16,18},{18... | collective-permute-start | bytes 98312 | tf_op jit(solution)/shard_map/ppermute | solution.py:51
  38.0 6.0 %collective-permute-start.5 = (bf16[128,128]{1,0:T(8,128)(2,1)S(1)}, bf16[128,128]{1,0:T(8,128)(2,1)S(1)}, u32[]{:S(2)}, u32[]{:S(2)}) collective-permute-start(bf16[128,128]{1,0:T(8,128)(2,1)S(1)} %collective-permute-done.4), channel_id=1, source_target_pairs={{0,2},{2,4},{4,6},{6,8},{8,10},{10,12},{12,14},{14,16},{16,18},{18... | collective-permute-start | bytes 98312 | tf_op jit(solution)/shard_map/ppermute | solution.py:51
  44.0 6.0 %collective-permute-start.6 = (bf16[128,128]{1,0:T(8,128)(2,1)S(1)}, bf16[128,128]{1,0:T(8,128)(2,1)S(1)}, u32[]{:S(2)}, u32[]{:S(2)}) collective-permute-start(bf16[128,128]{1,0:T(8,128)(2,1)S(1)} %collective-permute-done.5), channel_id=1, source_target_pairs={{0,2},{2,4},{4,6},{6,8},{8,10},{10,12},{12,14},{14,16},{16,18},{18... | collective-permute-start | bytes 98312 | tf_op jit(solution)/shard_map/ppermute | solution.py:51
  50.0 6.0 %collective-permute-start.7 = (bf16[128,128]{1,0:T(8,128)(2,1)S(1)}, bf16[128,128]{1,0:T(8,128)(2,1)S(1)}, u32[]{:S(2)}, u32[]{:S(2)}) collective-permute-start(bf16[128,128]{1,0:T(8,128)(2,1)S(1)} %collective-permute-done.6), channel_id=1, source_target_pairs={{0,2},{2,4},{4,6},{6,8},{8,10},{10,12},{12,14},{14,16},{16,18},{18... | collective-permute-start | bytes 98312 | tf_op jit(solution)/shard_map/ppermute | solution.py:51
  56.1 6.0 %collective-permute-start.8 = (bf16[128,128]{1,0:T(8,128)(2,1)S(1)}, bf16[128,128]{1,0:T(8,128)(2,1)S(1)}, u32[]{:S(2)}, u32[]{:S(2)}) collective-permute-start(bf16[128,128]{1,0:T(8,128)(2,1)S(1)} %collective-permute-done.7), channel_id=1, source_target_pairs={{0,2},{2,4},{4,6},{6,8},{8,10},{10,12},{12,14},{14,16},{16,18},{18... | collective-permute-start | bytes 98312 | tf_op jit(solution)/shard_map/ppermute | solution.py:51
  62.1 6.0 %collective-permute-start.9 = (bf16[128,128]{1,0:T(8,128)(2,1)S(1)}, bf16[128,128]{1,0:T(8,128)(2,1)S(1)}, u32[]{:S(2)}, u32[]{:S(2)}) collective-permute-start(bf16[128,128]{1,0:T(8,128)(2,1)S(1)} %collective-permute-done.8), channel_id=1, source_target_pairs={{0,2},{2,4},{4,6},{6,8},{8,10},{10,12},{12,14},{14,16},{16,18},{18... | collective-permute-start | bytes 98312 | tf_op jit(solution)/shard_map/ppermute | solution.py:51
  68.2 6.0 %collective-permute-start.10 = (bf16[128,128]{1,0:T(8,128)(2,1)S(1)}, bf16[128,128]{1,0:T(8,128)(2,1)S(1)}, u32[]{:S(2)}, u32[]{:S(2)}) collective-permute-start(bf16[128,128]{1,0:T(8,128)(2,1)S(1)} %collective-permute-done.9), channel_id=1, source_target_pairs={{0,2},{2,4},{4,6},{6,8},{8,10},{10,12},{12,14},{14,16},{16,18},{18... | collective-permute-start | bytes 98312 | tf_op jit(solution)/shard_map/ppermute | solution.py:51
  74.2 6.0 %collective-permute-start.11 = (bf16[128,128]{1,0:T(8,128)(2,1)S(1)}, bf16[128,128]{1,0:T(8,128)(2,1)S(1)}, u32[]{:S(2)}, u32[]{:S(2)}) collective-permute-start(bf16[128,128]{1,0:T(8,128)(2,1)S(1)} %collective-permute-done.10), channel_id=1, source_target_pairs={{0,2},{2,4},{4,6},{6,8},{8,10},{10,12},{12,14},{14,16},{16,18},{18... | collective-permute-start | bytes 98312 | tf_op jit(solution)/shard_map/ppermute | solution.py:51
  80.2 6.0 %collective-permute-start.12 = (bf16[128,128]{1,0:T(8,128)(2,1)S(1)}, bf16[128,128]{1,0:T(8,128)(2,1)S(1)}, u32[]{:S(2)}, u32[]{:S(2)}) collective-permute-start(bf16[128,128]{1,0:T(8,128)(2,1)S(1)} %collective-permute-done.11), channel_id=1, source_target_pairs={{0,2},{2,4},{4,6},{6,8},{8,10},{10,12},{12,14},{14,16},{16,18},{18... | collective-permute-start | bytes 98312 | tf_op jit(solution)/shard_map/ppermute | solution.py:51
  86.3 6.0 %collective-permute-start.13 = (bf16[128,128]{1,0:T(8,128)(2,1)S(1)}, bf16[128,128]{1,0:T(8,128)(2,1)S(1)}, u32[]{:S(2)}, u32[]{:S(2)}) collective-permute-start(bf16[128,128]{1,0:T(8,128)(2,1)S(1)} %collective-permute-done.12), channel_id=1, source_target_pairs={{0,2},{2,4},{4,6},{6,8},{8,10},{10,12},{12,14},{14,16},{16,18},{18... | collective-permute-start | bytes 98312 | tf_op jit(solution)/shard_map/ppermute | solution.py:51
  92.3 6.0 %collective-permute-start.14 = (bf16[128,128]{1,0:T(8,128)(2,1)S(1)}, bf16[128,128]{1,0:T(8,128)(2,1)S(1)}, u32[]{:S(2)}, u32[]{:S(2)}) collective-permute-start(bf16[128,128]{1,0:T(8,128)(2,1)S(1)} %collective-permute-done.13), channel_id=1, source_target_pairs={{0,2},{2,4},{4,6},{6,8},{8,10},{10,12},{12,14},{14,16},{16,18},{18... | collective-permute-start | bytes 98312 | tf_op jit(solution)/shard_map/ppermute | solution.py:51
  103.0 0.7 copy-start.2
  103.1 8.9 %copy-start.3 = (bf16[128,128]{1,0:T(8,128)(2,1)S(1)}, bf16[128,128]{1,0:T(8,128)(2,1)}, u32[]{:S(2)}) copy-start(bf16[128,128]{1,0:T(8,128)(2,1)} %param.11) | copy-start | bytes 98308
Sparse Core Ops, SparseCore 0:
  103.8 8.0 reduce-scatter.1
